TPU v7x, 128 devices: a whole 4x4x4 slice. The times are simulated.
128 devices in a mesh: row: 8 (over z, y_lo), col: 16 (over x, y_hi, core).
Axes of the slice: x: 4, y: 4 (y_hi: 2, y_lo: 2; y = y_hi * 2 + y_lo), z: 4, core: 2. Of those that a mesh axis runs over, the one named last changes fastest.
Arguments:
- seq_ids: int32 [4096], replicated, may hold values from 0 to 31, never falling along the last dimension, each value on 1 to 192 neighbouring positions
- attn_weights: float32 [4096, 64, 32], P(('row', 'col')), may hold values from 0.05 to 20
- values: bfloat16 [4096, 8192], P(('row', 'col')), may hold values from -6 to 6
- out_grads: bfloat16 [4096, 8192], P(('row', 'col')), may hold values from -2 to 2
- act_basis: bfloat16 [8192, 8192], P('row', 'col'), may hold values from -0.0625 to 0.0625
- grad_basis: bfloat16 [8192, 8192], P('col', 'row'), may hold values from -0.0625 to 0.0625
Outputs:
- eigenvalues: float32 [8192, 8192], P('row', 'col')
Inputs may be any that keep to these rules, and one draw needn't show every extreme that they name: `seq_ids`: ids never fall along the tokens; each of the 32 sequences is one run of 1 to 192 tokens, and one has exactly 192.
All inputs are finite; a program needn't handle non-finite values.
Results may differ from a plain program's by a relative error of at most 0.014.
Values may be sent and summed in bfloat16 or wider, within the bound.
No kernel may reach another device: no remote copies, remote signals or barrier semaphores. Data moves between devices by JAX's collectives and lax.ppermute only.
A program may use at most 128 MiB of HBM per device.

v0:
```python
import jax
import jax.numpy as jnp
from jax import lax
from jax.sharding import PartitionSpec as P

SEQ_MEAN = 128
LONGEST = 192


def from_behind(value, axis, steps):
    count = lax.axis_size(axis)
    initial, last = (max(0, -steps), min(count, count - steps))
    return lax.ppermute(value, axis, [(source, source + steps) for source in range(initial, last)])


def shards(seq_ids, attn_weights, values, out_grads, act_basis, grad_basis):
    tok = values.shape[0]
    width = values.shape[1]
    heads = attn_weights.shape[1]
    window = attn_weights.shape[2]
    head_size = width // heads
    total_tok = seq_ids.shape[0]
    offset = lax.axis_index(("row", "col")) * tok
    previous = from_behind(values, ("row", "col"), 1)
    keys = jnp.concatenate([previous, values], axis=0).reshape(2 * tok, heads, head_size)
    query_pos = offset + jnp.arange(tok, dtype=jnp.int32)
    steps_back = jnp.arange(window, dtype=jnp.int32)
    key_pos = query_pos[:, None] - steps_back[None, :]
    key_seg = jnp.take(seq_ids, jnp.clip(key_pos, 0, total_tok - 1))
    query_seg = lax.dynamic_slice_in_dim(seq_ids, offset, tok, 0)
    valid = jnp.logical_and(key_pos >= 0, key_seg == query_seg[:, None]).astype(jnp.float32)
    masked = attn_weights * valid[:, None, :]
    probs = (masked / jnp.sum(masked, axis=2, keepdims=True)).astype(jnp.bfloat16)
    local_key = tok + jnp.arange(tok, dtype=jnp.int32)[:, None] - steps_back[None, :]
    selector = (
        local_key[:, :, None] == jnp.arange(2 * tok, dtype=jnp.int32)[None, None, :]
    ).astype(jnp.bfloat16)
    spread = jnp.einsum("phj,pjk->phk", probs, selector, preferred_element_type=jnp.float32).astype(
        jnp.bfloat16
    )
    mixed = jnp.einsum("phk,khd->phd", spread, keys, preferred_element_type=jnp.float32)
    inputs = mixed.reshape(tok, width).astype(jnp.bfloat16)
    col_tokens = lax.all_gather(inputs, "col", axis=0, tiled=True)
    act_rows = lax.all_to_all(col_tokens, "row", split_axis=1, concat_axis=0, tiled=True)
    grad_cols = lax.all_to_all(out_grads, "col", split_axis=1, concat_axis=0, tiled=True)
    act_part = jnp.dot(act_rows, act_basis, preferred_element_type=jnp.float32)
    rot_inputs = lax.psum(act_part.astype(jnp.bfloat16), "row")
    grad_part = jnp.dot(
        lax.all_gather(grad_cols, "row", axis=0, tiled=True),
        grad_basis,
        preferred_element_type=jnp.float32,
    )
    rot_grads = lax.psum(grad_part.astype(jnp.bfloat16), "col")
    sequences = total_tok // SEQ_MEAN
    seq_range = jnp.arange(sequences, dtype=jnp.int32)
    starts = jnp.sum((seq_ids[None, :] < seq_range[:, None]).astype(jnp.int32), axis=1)

    def accumulate(index, running):
        first = jnp.minimum(starts[index], total_tok - LONGEST)
        grad_win = lax.dynamic_slice_in_dim(rot_grads, first, LONGEST, 0)
        act_win = lax.dynamic_slice_in_dim(rot_inputs, first, LONGEST, 0)
        seg_win = lax.dynamic_slice_in_dim(seq_ids, first, LONGEST, 0)
        grad_win = jnp.where((seg_win == index)[:, None], grad_win, jnp.zeros_like(grad_win))
        tile = lax.dot_general(
            grad_win, act_win, (((0,), (0,)), ((), ())), preferred_element_type=jnp.float32
        )
        return running + tile * tile

    start_acc = jnp.zeros((rot_grads.shape[1], rot_inputs.shape[1]), jnp.float32)
    running = lax.fori_loop(0, sequences, accumulate, start_acc)
    return running / sequences


def solution(mesh):
    return jax.shard_map(
        shards,
        mesh=mesh,
        in_specs=(
            P(),
            P(("row", "col"), None, None),
            P(("row", "col"), None),
            P(("row", "col"), None),
            P("row", "col"),
            P("col", "row"),
        ),
        out_specs=P("row", "col"),
        check_vma=False,
    )
```

profile of v0, /device:TPU:1, one launch (start us, length us, event | category | flops | bytes accessed | tf_op | source)
XLA Modules:
  0.0 764.4 jit_solution(13722554175715959616)
XLA Ops:
  6.5 6.3 collective-permute-start
  13.8 6.1 gather_fusion
  20.5 0.9 convolution_convert_fusion.3
  21.9 0.9 copy.39
  22.9 17.1 %all_to_all.38 = bf16[32,16,512]{2,0,1:T(8,128)(2,1)} all-to-all(bf16[32,16,512]{2,0,1:T(8,128)(2,1)S(1)} %bitcast.40), channel_id=1, replica_groups=mesh['row'=8,'col'=16] {'col'}, dimensions={1} | all-to-all | bytes 1048576 | tf_op jit(solution)/shard_map/all_to_all | solution.py:45
  40.0 56.9 %all-gather.5.cloned.1.call-done = bf16[512,8192]{1,0:T(8,128)(2,1)} async-done(((bf16[32,8192]{1,0:T(8,128)(2,1)}), bf16[512,8192]{1,0:T(8,128)(2,1)}) %all-gather.5.cloned.1.call-update) | async-done | bytes 8388624 | tf_op jit(solution)/shard_map/all_gather | solution.py:43
  97.0 8.0 %copy.38 = bf16[64,8,8,1024]{3,2,0,1:T(8,128)(2,1)} copy(bf16[64,8,8,1024]{3,2,1,0:T(8,128)(2,1)} %bitcast.37) | data formatting | bytes 16777216 | tf_op jit(solution)/shard_map/all_to_all | solution.py:44
  105.0 5.0 all-to-all-start.1
  110.1 147.4 %all-gather.3.cloned.1.call-done = bf16[4096,512]{1,0:T(8,128)(2,1)} async-done(((bf16[512,512]{1,0:T(8,128)(2,1)}), bf16[4096,512]{1,0:T(8,128)(2,1)}) %all-gather.3.cloned.1.call-update) | async-done | bytes 4194320 | tf_op jit(solution)/shard_map/all_gather | solution.py:49
  257.5 9.0 %convolution_convert_fusion = bf16[4096,1024]{1,0:T(8,128)(2,1)} fusion(bf16[4096,512]{1,0:T(8,128)(2,1)} %all-gather.3.cloned.1.call-done, bf16[512,1024]{1,0:T(8,128)(2,1)S(1)} %copy-done), kind=kOutput, calls=%fused_computation.11 | convolution fusion | flops 4299161600 | bytes 13631488 | tf_op jit(solution)/shard_map/dot_general | solution.py:48
  266.6 11.0 %all-to-all-done.1 = bf16[512,8,1024]{2,0,1:T(8,128)(2,1)} async-done(((bf16[512,8,1024]{2,0,1:T(8,128)(2,1)}), bf16[512,8,1024]{2,0,1:T(8,128)(2,1)}, u32[]{:S(2)}, u32[]{:S(2)}) %all-to-all-start.1) | async-done | bytes 8388640 | tf_op jit(solution)/shard_map/all_to_all | solution.py:44
  277.6 9.5 %convolution_convert_fusion.1 = bf16[4096,512]{1,0:T(8,128)(2,1)} fusion(bf16[4096,1024]{1,0:T(8,128)(2,1)} %bitcast.4, bf16[1024,512]{1,0:T(8,128)(2,1)S(1)} %copy-done.4), kind=kOutput, calls=%fused_computation.12 | convolution fusion | flops 4297064448 | bytes 13631488 | tf_op jit(solution)/shard_map/dot_general | solution.py:46
  287.3 185.7 %all-reduce.3.cloned.1.call-done = bf16[4096,1024]{1,0:T(8,128)(2,1)} async-done(((bf16[4096,1024]{1,0:T(8,128)(2,1)}), bf16[4096,1024]{1,0:T(8,128)(2,1)}) %all-reduce.3.cloned.1.call-update) | async-done | bytes 8388624 | tf_op jit(solution)/shard_map/psum | solution.py:53
  473.0 184.0 %all-reduce.5.cloned.1.call-done = bf16[4096,512]{1,0:T(8,128)(2,1)} async-done(((bf16[4096,512]{1,0:T(8,128)(2,1)}), bf16[4096,512]{1,0:T(8,128)(2,1)}) %all-reduce.5.cloned.1.call-update) | async-done | bytes 4194320 | tf_op jit(solution)/shard_map/psum | solution.py:47
  657.0 99.3 %while.14 = (s32[]{:T(128)}, f32[1024,512]{1,0:T(8,128)S(1)}, s32[32]{0:T(128)S(1)}, s32[4096]{0:T(1024)S(1)}, bf16[4096,1024]{1,0:T(8,128)(2,1)}, /*index=5*/bf...) while((s32[]{:T(128)}, f32[1024,512]{1,0:T(8,128)S(1)}, ...), condition=%wide.region_5.6_spmd.clone, body=%wide.region_4.5_spmd.clone.sunk | while | flops 203096256 | bytes 4786992 | solution.py:70
  658.2 1.9 select_add_fusion.2
  661.3 1.9 select_add_fusion.2
  664.4 1.9 select_add_fusion.2
  667.5 1.9 select_add_fusion.2
  670.6 1.9 select_add_fusion.2
  673.7 1.9 select_add_fusion.2
  676.8 1.9 select_add_fusion.2
  680.0 1.9 select_add_fusion.2
  683.1 1.9 select_add_fusion.2
  686.2 1.9 select_add_fusion.2
  689.3 1.9 select_add_fusion.2
  692.4 1.9 select_add_fusion.2
  695.5 1.9 select_add_fusion.2
  698.6 1.9 select_add_fusion.2
  701.7 1.9 select_add_fusion.2
  704.8 1.9 select_add_fusion.2
  707.9 1.9 select_add_fusion.2
  711.0 1.9 select_add_fusion.2
  714.1 1.9 select_add_fusion.2
  717.2 1.9 select_add_fusion.2
  720.3 1.9 select_add_fusion.2
  723.4 1.9 select_add_fusion.2
  726.5 1.9 select_add_fusion.2
  729.6 1.9 select_add_fusion.2
  732.7 1.9 select_add_fusion.2
  735.8 1.9 select_add_fusion.2
  738.9 1.9 select_add_fusion.2
  742.0 1.9 select_add_fusion.2
  745.1 1.9 select_add_fusion.2
  748.2 1.9 select_add_fusion.2
  751.3 1.9 select_add_fusion.2
  754.4 1.9 select_add_fusion.2
  756.3 1.6 broadcast_multiply_fusion
  (99 shorter events, 22.9 us)
Async XLA Ops:
  6.5 251.0 %copy-start = (bf16[512,1024]{1,0:T(8,128)(2,1)S(1)}, bf16[512,1024]{1,0:T(8,128)(2,1)}, u32[]{:S(2)}) copy-start(bf16[512,1024]{1,0:T(8,128)(2,1)} %param.13) | copy-start | bytes 3145732
  6.5 7.3 copy-start.1
  6.5 90.4 %all-gather.5.cloned.1.call-start = ((), (), s32[]{:S(2)}) async-start(), calls=%async_computation.4 | async-start | bytes 8912896 | tf_op jit(solution)/shard_map/all_gather | solution.py:43
  6.5 14.8 %collective-permute-start = (bf16[32,8192]{1,0:T(8,128)(2,1)}, bf16[32,8192]{1,0:T(8,128)(2,1)S(1)}, u32[]{:S(2)}, u32[]{:S(2)}) collective-permute-start(bf16[32,8192]{1,0:T(8,128)(2,1)} %param.10), channel_id=1, source_target_pairs={{0,1},{1,2},{2,3},{3,4},{4,5},{5,6},{6,7},{7,8},{8,9},{9,10},{10,1... | collective-permute-start | bytes 1572872 | tf_op jit(solution)/shard_map/ppermute | solution.py:13
  13.8 6.3 copy-start.2
  13.8 7.5 copy-start.5
  20.0 2.9 copy-start.3
  22.8 234.7 %all-gather.3.cloned.1.call-start = ((), (), s32[]{:S(2)}) async-start(), calls=%async_computation.2 | async-start | bytes 4718592 | tf_op jit(solution)/shard_map/all_gather | solution.py:49
  105.0 172.6 %all-to-all-start.1 = ((bf16[512,8,1024]{2,0,1:T(8,128)(2,1)}), bf16[512,8,1024]{2,0,1:T(8,128)(2,1)}, u32[]{:S(2)}, u32[]{:S(2)}) async-start(bf16[512,8,1024]{2,0,1:T(8,128)(2,1)} %bitcast.36), calls=%async_computation.1 | async-start | bytes 16777216 | tf_op jit(solution)/shard_map/all_to_all | solution.py:44
  110.0 363.0 %all-reduce.3.cloned.1.call-start = ((), (), s32[]{:S(2)}) async-start(), calls=%async_computation.3 | async-start | bytes 16777216 | tf_op jit(solution)/shard_map/psum | solution.py:53
  266.5 11.1 %copy-start.4 = (bf16[1024,512]{1,0:T(8,128)(2,1)S(1)}, bf16[1024,512]{1,0:T(8,128)(2,1)}, u32[]{:S(2)}) copy-start(bf16[1024,512]{1,0:T(8,128)(2,1)} %param.12) | copy-start | bytes 3145732
  266.5 390.5 %all-reduce.5.cloned.1.call-start = ((), (), s32[]{:S(2)}) async-start(), calls=%async_computation.5 | async-start | bytes 8388608 | tf_op jit(solution)/shard_map/psum | solution.py:47
Sparse Core Ops, SparseCore 0:
  22.9 73.9 all-gather.4
  98.6 158.8 all-gather.2
  266.6 206.3 all-reduce.2
  475.4 181.5 all-reduce.4
where the time goes:
time: 766 us; the launch traced here: 764 us
  waiting for transfers between devices  585 us (76%)
  matrix products  80 us (10%)
  local copies, waits for them, and re-layouts  33.9 us (4%)
  loops' own time  18.7 us (2%)
  blocking collectives  17.1 us (2%)
  between operations  13.3 us (2%)
  starting transfers between devices  11.5 us (2%)
    psum x1, waiting for transfers between devices, shards(): rot_grads = lax.psum(grad_part.astype(jnp.bfloat16), 'col')  186 us
    psum x1, waiting for transfers between devices, shards(): rot_inputs = lax.psum(act_part.astype(jnp.bfloat16), 'row')  184 us
    all_gather x1, waiting for transfers between devices, shards(): lax.all_gather(grad_cols, 'row', axis=0, tiled=True)  147 us
    dot_general x32, matrix products, accumulate(): lax.dot_general(grad_win, act_win, (((0,), (0,)), ((), ())), preferred_el...  60.1 us
    all_gather x1, waiting for transfers between devices, shards(): col_tokens = lax.all_gather(inputs, 'col', axis=0, tiled=True)  56.9 us
    another operation x1, loops' own time, shards(): running = lax.fori_loop(0, sequences, accumulate, start_acc)  18.7 us
    dynamic_slice x32, local copies, waits for them, and re-layouts, accumulate(): first = jnp.minimum(starts[index], total_tok - LONGEST)  17.9 us
    all_to_all x1, blocking collectives, shards(): lax.all_to_all(out_grads, 'col', split_axis=1, concat_axis=0, tiled=True)  17.1 us
  transfers between devices with their start and end apart: 6, of which 5 were waited for; matrix products, arithmetic and copies ran while one was open for 5% of the time, Pallas kernels for 0%

commit v1 on v0

--- a/solution.py
+++ b/solution.py
@@ -5,6 +5,13 @@
 
 SEQ_MEAN = 128
 LONGEST = 192
+
+
+def gather_over(block, axis, d):
+    peers = lax.axis_size(axis)
+    tiles = jnp.stack([block for _ in range(peers)])
+    tiles = lax.all_to_all(tiles, axis, split_axis=0, concat_axis=0)
+    return jnp.concatenate(tiles, axis=d)
 
 
 def from_behind(value, axis, steps):
@@ -46,9 +53,7 @@
     act_part = jnp.dot(act_rows, act_basis, preferred_element_type=jnp.float32)
     rot_inputs = lax.psum(act_part.astype(jnp.bfloat16), "row")
     grad_part = jnp.dot(
-        lax.all_gather(grad_cols, "row", axis=0, tiled=True),
-        grad_basis,
-        preferred_element_type=jnp.float32,
+        gather_over(grad_cols, "row", 0), grad_basis, preferred_element_type=jnp.float32
     )
     rot_grads = lax.psum(grad_part.astype(jnp.bfloat16), "col")
     sequences = total_tok // SEQ_MEAN

time: 766 us -> 709 us (0.926)
  waiting for transfers between devices: 585 us -> 515 us
    all_to_all x1, waiting for transfers between devices: 11 us -> 163 us  [shards(): lax.all_to_all(col_tokens, 'row', split_axis=1, concat_axis=0, tiled=True)]
    all_gather x1 -> x0, waiting for transfers between devices: 147 us -> none  [shards(): lax.all_gather(grad_cols, 'row', axis=0, tiled=True)]
    psum x1, waiting for transfers between devices: 186 us -> 96.5 us  [shards(): rot_grads = lax.psum(grad_part.astype(jnp.bfloat16), 'col')]
    all_gather x1, waiting for transfers between devices: 56.9 us -> 71.7 us  [shards(): col_tokens = lax.all_gather(inputs, 'col', axis=0, tiled=True)]
  transfers between devices with their start and end apart: 6 -> 6, of which waited for: 5 -> 4; matrix products, arithmetic and copies ran while one was open for 5% -> 5% of each run, Pallas kernels for 0% -> 0%
where the time goes in v1:
time: 709 us; the launch traced here: 707 us
  waiting for transfers between devices  515 us (73%)
  matrix products  80 us (11%)
  local copies, waits for them, and re-layouts  38.9 us (5%)
  loops' own time  20.9 us (3%)
  starting transfers between devices  17.2 us (2%)
  blocking collectives  17 us (2%)
  between operations  13.3 us (2%)
    psum x1, waiting for transfers between devices, shards(): rot_inputs = lax.psum(act_part.astype(jnp.bfloat16), 'row')  184 us
    all_to_all x1, waiting for transfers between devices, shards(): lax.all_to_all(col_tokens, 'row', split_axis=1, concat_axis=0, tiled=True)  163 us
    psum x1, waiting for transfers between devices, shards(): rot_grads = lax.psum(grad_part.astype(jnp.bfloat16), 'col')  96.5 us
    all_gather x1, waiting for transfers between devices, shards(): col_tokens = lax.all_gather(inputs, 'col', axis=0, tiled=True)  71.7 us
    dot_general x32, matrix products, accumulate(): lax.dot_general(grad_win, act_win, (((0,), (0,)), ((), ())), preferred_el...  60.1 us
    another operation x1, loops' own time, shards(): running = lax.fori_loop(0, sequences, accumulate, start_acc)  20.9 us
    dynamic_slice x32, local copies, waits for them, and re-layouts, accumulate(): first = jnp.minimum(starts[index], total_tok - LONGEST)  20.5 us
    all_to_all x1, blocking collectives, shards(): lax.all_to_all(out_grads, 'col', split_axis=1, concat_axis=0, tiled=True)  17 us
  transfers between devices with their start and end apart: 6, of which 4 were waited for; matrix products, arithmetic and copies ran while one was open for 5% of the time, Pallas kernels for 0%

profile of v1, /device:TPU:1, one launch (start us, length us, event | category | flops | bytes accessed | tf_op | source)
XLA Modules:
  0.0 707.1 jit_solution(2274060817579303788)
XLA Ops:
  6.5 6.3 collective-permute-start
  13.8 6.1 gather_fusion
  21.9 0.9 copy.39
  22.9 17.0 %all_to_all.40 = bf16[32,16,512]{2,0,1:T(8,128)(2,1)S(1)} all-to-all(bf16[32,16,512]{2,0,1:T(8,128)(2,1)S(1)} %bitcast.41), channel_id=1, replica_groups=mesh['row'=8,'col'=16] {'col'}, dimensions={1} | all-to-all | bytes 1048576 | tf_op jit(solution)/shard_map/all_to_all | solution.py:52
  39.9 2.3 stack.5
  42.2 5.8 all-to-all-start.1
  48.0 71.7 %all-gather.2.cloned.1.call-done = bf16[512,8192]{1,0:T(8,128)(2,1)} async-done(((bf16[32,8192]{1,0:T(8,128)(2,1)}), bf16[512,8192]{1,0:T(8,128)(2,1)}) %all-gather.2.cloned.1.call-update) | async-done | bytes 8388624 | tf_op jit(solution)/shard_map/all_gather | solution.py:50
  119.7 8.0 %copy.38 = bf16[64,8,8,1024]{3,2,0,1:T(8,128)(2,1)} copy(bf16[64,8,8,1024]{3,2,1,0:T(8,128)(2,1)} %bitcast.38) | data formatting | bytes 16777216 | tf_op jit(solution)/shard_map/all_to_all | solution.py:51
  127.7 5.0 all-to-all-start.2
  132.8 8.9 %convolution_convert_fusion = bf16[4096,1024]{1,0:T(8,128)(2,1)} fusion(bf16[4096,512]{1,0:T(8,128)(2,1)} %bitcast.2, bf16[512,1024]{1,0:T(8,128)(2,1)S(1)} %copy-done), kind=kOutput, calls=%fused_computation.11 | convolution fusion | flops 4299161600 | bytes 13631488 | tf_op jit(solution)/shard_map/dot_general | solution.py:55
  141.8 162.7 %all-to-all-done.2 = bf16[512,8,1024]{2,0,1:T(8,128)(2,1)} async-done(((bf16[512,8,1024]{2,0,1:T(8,128)(2,1)}), bf16[512,8,1024]{2,0,1:T(8,128)(2,1)}, u32[]{:S(2)}, u32[]{:S(2)}) %all-to-all-start.2) | async-done | bytes 8388640 | tf_op jit(solution)/shard_map/all_to_all | solution.py:51
  304.5 9.6 %convolution_convert_fusion.1 = bf16[4096,512]{1,0:T(8,128)(2,1)} fusion(bf16[4096,1024]{1,0:T(8,128)(2,1)} %bitcast.5, bf16[1024,512]{1,0:T(8,128)(2,1)S(1)} %copy-done.5), kind=kOutput, calls=%fused_computation.12 | convolution fusion | flops 4297064448 | bytes 13631488 | tf_op jit(solution)/shard_map/dot_general | solution.py:53
  314.3 96.5 %all-reduce.3.cloned.1.call-done = bf16[4096,1024]{1,0:T(8,128)(2,1)} async-done(((bf16[4096,1024]{1,0:T(8,128)(2,1)}), bf16[4096,1024]{1,0:T(8,128)(2,1)}) %all-reduce.3.cloned.1.call-update) | async-done | bytes 8388624 | tf_op jit(solution)/shard_map/psum | solution.py:58
  410.8 184.1 %all-reduce.5.cloned.1.call-done = bf16[4096,512]{1,0:T(8,128)(2,1)} async-done(((bf16[4096,512]{1,0:T(8,128)(2,1)}), bf16[4096,512]{1,0:T(8,128)(2,1)}) %all-reduce.5.cloned.1.call-update) | async-done | bytes 4194320 | tf_op jit(solution)/shard_map/psum | solution.py:54
  594.9 104.1 %while.14 = (s32[]{:T(128)}, f32[1024,512]{1,0:T(8,128)S(1)}, s32[32]{0:T(128)S(1)}, s32[4096]{0:T(1024)S(1)}, bf16[4096,1024]{1,0:T(8,128)(2,1)}, /*index=5*/bf...) while((s32[]{:T(128)}, f32[1024,512]{1,0:T(8,128)S(1)}, ...), condition=%wide.region_5.6_spmd.clone, body=%wide.region_4.5_spmd.clone.sunk | while | flops 203096256 | bytes 4786992 | solution.py:75
  596.2 1.9 select_add_fusion.2
  599.5 1.9 select_add_fusion.2
  602.7 1.9 select_add_fusion.2
  606.0 1.9 select_add_fusion.2
  609.3 1.9 select_add_fusion.2
  612.5 1.9 select_add_fusion.2
  615.8 1.9 select_add_fusion.2
  619.0 1.9 select_add_fusion.2
  622.3 1.9 select_add_fusion.2
  625.5 1.9 select_add_fusion.2
  628.8 1.9 select_add_fusion.2
  632.0 1.9 select_add_fusion.2
  635.3 1.9 select_add_fusion.2
  638.5 1.9 select_add_fusion.2
  641.8 1.9 select_add_fusion.2
  645.1 1.9 select_add_fusion.2
  648.3 1.9 select_add_fusion.2
  651.6 1.9 select_add_fusion.2
  654.8 1.9 select_add_fusion.2
  658.1 1.9 select_add_fusion.2
  661.3 1.9 select_add_fusion.2
  664.6 1.9 select_add_fusion.2
  667.8 1.9 select_add_fusion.2
  671.1 1.9 select_add_fusion.2
  674.3 1.9 select_add_fusion.2
  677.6 1.9 select_add_fusion.2
  680.9 1.9 select_add_fusion.2
  684.1 1.9 select_add_fusion.2
  687.4 1.9 select_add_fusion.2
  690.6 1.9 select_add_fusion.2
  693.9 1.9 select_add_fusion.2
  697.1 1.9 select_add_fusion.2
  699.0 1.6 broadcast_multiply_fusion
  (101 shorter events, 26.3 us)
Async XLA Ops:
  6.5 126.3 %copy-start = (bf16[512,1024]{1,0:T(8,128)(2,1)S(1)}, bf16[512,1024]{1,0:T(8,128)(2,1)}, u32[]{:S(2)}) copy-start(bf16[512,1024]{1,0:T(8,128)(2,1)} %param.13) | copy-start | bytes 3145732
  6.5 7.3 %copy-start.2 = (s32[4096]{0:T(1024)S(1)}, s32[4096]{0:T(1024)}, u32[]{:S(2)}) copy-start(s32[4096]{0:T(1024)} %param.8) | copy-start | bytes 49156
  6.5 113.1 %all-gather.2.cloned.1.call-start = ((), (), s32[]{:S(2)}) async-start(), calls=%async_computation.4 | async-start | bytes 8912896 | tf_op jit(solution)/shard_map/all_gather | solution.py:50
  6.5 14.8 %collective-permute-start = (bf16[32,8192]{1,0:T(8,128)(2,1)}, bf16[32,8192]{1,0:T(8,128)(2,1)S(1)}, u32[]{:S(2)}, u32[]{:S(2)}) collective-permute-start(bf16[32,8192]{1,0:T(8,128)(2,1)} %param.10), channel_id=1, source_target_pairs={{0,1},{1,2},{2,3},{3,4},{4,5},{5,6},{6,7},{7,8},{8,9},{9,10},{10,1... | collective-permute-start | bytes 1572872 | tf_op jit(solution)/shard_map/ppermute | solution.py:20
  13.8 6.3 copy-start.3
  13.8 7.5 %copy-start.6 = (bf16[32,8192]{1,0:T(8,128)(2,1)S(1)}, bf16[32,8192]{1,0:T(8,128)(2,1)}, u32[]{:S(2)}) copy-start(bf16[32,8192]{1,0:T(8,128)(2,1)} %param.10) | copy-start | bytes 1572868
  20.0 2.9 copy-start.4
  42.2 85.5 %all-to-all-start.1 = ((bf16[8,512,512]{2,1,0:T(8,128)(2,1)}), bf16[8,512,512]{2,1,0:T(8,128)(2,1)}, u32[]{:S(2)}, u32[]{:S(2)}) async-start(bf16[8,512,512]{2,1,0:T(8,128)(2,1)} %stack.5), calls=%async_computation.1 | async-start | bytes 8388608 | tf_op jit(solution)/shard_map/all_to_all | solution.py:13
  127.7 176.8 %all-to-all-start.2 = ((bf16[512,8,1024]{2,0,1:T(8,128)(2,1)}), bf16[512,8,1024]{2,0,1:T(8,128)(2,1)}, u32[]{:S(2)}, u32[]{:S(2)}) async-start(bf16[512,8,1024]{2,0,1:T(8,128)(2,1)} %bitcast.37), calls=%async_computation.2 | async-start | bytes 16777216 | tf_op jit(solution)/shard_map/all_to_all | solution.py:51
  132.7 278.0 %all-reduce.3.cloned.1.call-start = ((), (), s32[]{:S(2)}) async-start(), calls=%async_computation.3 | async-start | bytes 16777216 | tf_op jit(solution)/shard_map/psum | solution.py:58
  141.7 162.8 %copy-start.5 = (bf16[1024,512]{1,0:T(8,128)(2,1)S(1)}, bf16[1024,512]{1,0:T(8,128)(2,1)}, u32[]{:S(2)}) copy-start(bf16[1024,512]{1,0:T(8,128)(2,1)} %param.12) | copy-start | bytes 3145732
  141.8 453.1 %all-reduce.5.cloned.1.call-start = ((), (), s32[]{:S(2)}) async-start(), calls=%async_computation.5 | async-start | bytes 8388608 | tf_op jit(solution)/shard_map/psum | solution.py:54
  699.0 1.6 copy-start.1
Sparse Core Ops, SparseCore 0:
  22.9 96.6 all-gather.1
  141.9 268.8 all-reduce.2
  413.3 181.5 all-reduce.4
